TPU v7x, 128 devices: a whole 4x4x4 slice. The times are simulated.
128 devices in a mesh: teacher: 4 (over y_hi, core), seq: 32 (over x, y_lo, z).
Axes of the slice: x: 4, y: 4 (y_hi: 2, y_lo: 2; y = y_hi * 2 + y_lo), z: 4, core: 2. Of those that a mesh axis runs over, the one named last changes fastest.
Arguments:
- activations: bfloat16 [20, 2048, 1536], P('teacher', 'seq'), may hold values from -150 to 150
- teacher_maps: bfloat16 [4, 20, 2048, 1536], P('teacher', None, 'seq'), may hold values from -6 to 6
- projection: bfloat16 [4, 1536, 1536], P('teacher', 'seq'), may hold values from -0.625 to 0.625
- dilated_weight: bfloat16 [1536, 3, 768], P('seq'), may hold values from -0.09375 to 0.09375
- pointwise_weight: bfloat16 [768, 1536], P('seq'), may hold values from -0.21875 to 0.21875
Outputs:
- loss_mean: float32 [], replicated
- dilated_grad: float32 [1536, 3, 768], P('seq')
- pointwise_grad: float32 [768, 1536], P('seq')
All inputs are finite; a program needn't handle non-finite values.
Results may differ from a plain program's by a relative error of at most 0.00081.
Values may be sent and summed in bfloat16 or wider, within the bound.
No kernel may reach another device: no remote copies, remote signals or barrier semaphores. Data moves between devices by JAX's collectives and lax.ppermute only.
A program may use at most 128 MiB of HBM per device.

v0:
```python
import jax
import jax.numpy as jnp
from jax import lax
from jax.sharding import PartitionSpec as P

TAP_DILATION = 16
slope_const = 0.7978845608
cubic_const = 0.044715


def padded(block, sides, width):
    for axis, dim in sides:
        count = lax.axis_size(axis)
        forward = [(i, i + 1) for i in range(count - 1)]
        backward = [(target, source) for source, target in forward]
        low = lax.ppermute(
            lax.slice_in_dim(block, block.shape[dim] - width, None, axis=dim), axis, forward
        )
        high = lax.ppermute(lax.slice_in_dim(block, 0, width, axis=dim), axis, backward)
        block = jnp.concatenate([low, block, high], axis=dim)
    return block


def gelu_tanh(value):
    inside = slope_const * (value + cubic_const * value * value * value)
    return 0.5 * value * (1.0 + jnp.tanh(inside))


def gelu_slope(value):
    inside = slope_const * (value + cubic_const * value * value * value)
    tangent = jnp.tanh(inside)
    return 0.5 * (1.0 + tangent) + 0.5 * value * (1.0 - tangent * tangent) * slope_const * (
        1.0 + 3.0 * cubic_const * value * value
    )


def column_product(left, right):
    return lax.dot_general(
        left, right, (((0,), (0,)), ((), ())), preferred_element_type=jnp.float32
    )


def shards(activations, teacher_maps, projection, dilated_weight, pointwise_weight):
    groups = lax.axis_size("teacher")
    ranks = lax.axis_size("seq")
    win_grp, bins_per_device, channel_count = activations.shape
    branch_width = dilated_weight.shape[2]
    count_of_rows = win_grp * bins_per_device
    total_rows = count_of_rows * groups * ranks
    maps_flat = teacher_maps[0].reshape(-1, teacher_maps.shape[3])
    columns = maps_flat
    projected = jnp.dot(
        columns,
        lax.all_gather(projection, "seq", axis=1, tiled=True)[0],
        preferred_element_type=jnp.float32,
    )
    projected = lax.optimization_barrier(projected.astype(jnp.bfloat16)).astype(jnp.float32)
    summed = lax.psum(projected, "teacher")
    own_rows = lax.dynamic_slice_in_dim(
        summed, lax.axis_index("teacher") * count_of_rows, count_of_rows, 0
    )
    target = own_rows / groups
    inputs_f = activations.reshape(count_of_rows, channel_count).astype(jnp.float32)
    sum_first, sum_second = lax.psum(
        (jnp.sum(inputs_f, axis=0), jnp.sum(inputs_f * inputs_f, axis=0)), ("teacher", "seq")
    )
    channel_mean = sum_first / total_rows
    channel_var = sum_second / total_rows - channel_mean * channel_mean
    normed = (inputs_f - channel_mean) * lax.rsqrt(channel_var + 1e-05)
    hidden_state = (
        gelu_tanh(normed).astype(jnp.bfloat16).reshape(win_grp, bins_per_device, channel_count)
    )
    padded_input = padded(hidden_state, (("seq", 1),), TAP_DILATION)
    tap_weights = [
        padded_input[
            :, offset_index * TAP_DILATION : offset_index * TAP_DILATION + bins_per_device
        ].reshape(count_of_rows, channel_count)
        for offset_index in range(3)
    ]
    running = jnp.zeros((count_of_rows, branch_width), jnp.float32)
    section = lax.all_gather(dilated_weight, "seq", axis=0, tiled=True)
    for offset_index in range(3):
        columns = tap_weights[offset_index]
        running = running + jnp.dot(
            columns, section[:, offset_index, :], preferred_element_type=jnp.float32
        )
    activated = gelu_tanh(running).astype(jnp.bfloat16)
    pointwise_full = lax.all_gather(pointwise_weight, "seq", axis=0, tiled=True)
    student = inputs_f + jnp.dot(activated, pointwise_full, preferred_element_type=jnp.float32)
    misfit = student - target
    squared_total = lax.psum(jnp.sum(misfit * misfit), ("teacher", "seq"))
    loss_mean = 0.5 * squared_total / (channel_count * total_rows)
    out_grad = (misfit / channel_count).astype(jnp.bfloat16)
    back_grad = lax.dot_general(
        out_grad, pointwise_full, (((1,), (1,)), ((), ())), preferred_element_type=jnp.float32
    )
    preact_grad = (back_grad * gelu_slope(running)).astype(jnp.bfloat16)
    dilated_part = lax.psum_scatter(
        jnp.stack(
            [column_product(tap_weights[offset_index], preact_grad) for offset_index in range(3)],
            axis=1,
        ),
        "seq",
        scatter_dimension=0,
        tiled=True,
    )
    pointwise_part = lax.psum_scatter(
        column_product(activated, out_grad), "seq", scatter_dimension=0, tiled=True
    )
    dilated_grad, pointwise_grad = lax.psum((dilated_part, pointwise_part), "teacher")
    return (loss_mean, dilated_grad, pointwise_grad)


def solution(mesh):
    in_specs = (
        P("teacher", "seq", None),
        P("teacher", None, "seq", None),
        P("teacher", "seq", None),
        P("seq", None, None),
        P("seq", None),
    )
    out_specs = (P(), P("seq", None, None), P("seq", None))
    return jax.shard_map(shards, mesh=mesh, in_specs=in_specs, out_specs=out_specs, check_vma=False)
```

profile of v0, /device:TPU:1, one launch (start us, length us, event | category | flops | bytes accessed | tf_op | source)
XLA Modules:
  0.0 940.9 jit_solution(16138648876742079881)
XLA Ops:
  7.2 0.0 copy-start
  7.2 0.0 all-gather.8.cloned.1.call-start
  7.2 0.7 all-gather.8.cloned.1.call-update
  7.9 0.0 all-gather.4.cloned.1.call-start
  8.0 0.7 all-gather.4.cloned.1.call-update
  8.7 0.0 all-gather.6.cloned.1.call-start
  8.7 1.5 convert_reduce_fusion
  10.2 71.5 %all-reduce = (f32[1536]{0:T(1024)S(1)}, f32[1536]{0:T(1024)S(1)}) all-reduce(f32[1536]{0:T(1024)S(1)} %get-tuple-element.4, f32[1536]{0:T(1024)S(1)} %get-tuple-element.3), channel_id=1, replica_groups=mesh['teacher'=4,'seq'=32] {'teacher','seq'}, use_global_device_ids=true, to_apply=%region_3.0 | all-reduce | flops 3072 | bytes 24576 | tf_op jit(solution)/shard_map/psum | solution.py:64
  81.7 0.0 copy-done
  81.7 0.8 fusion.9
  82.6 1.3 collective-permute-start
  83.9 1.3 collective-permute-start.1
  85.2 0.0 all-gather.6.cloned.1.call-update
  85.2 0.0 reduce-scatter.5.cloned.1.call-start
  85.3 5.7 collective-permute-done
  91.0 4.3 collective-permute-done.1
  95.2 1.2 pad_maximum_fusion.2
  96.4 54.6 %all-gather.8.cloned.1.call-done = bf16[1,1536,1536]{2,1,0:T(8,128)(2,1)} async-done(((bf16[1,48,1536]{2,1,0:T(8,128)(2,1)}), bf16[1,1536,1536]{2,1,0:T(8,128)(2,1)}) %all-gather.8.cloned.1.call-update) | async-done | bytes 4718608 | tf_op jit(solution)/shard_map/all_gather | solution.py:54
  151.0 10.7 %convolution_convert_fusion = bf16[1280,1536]{1,0:T(8,128)(2,1)} fusion(bf16[1280,1536]{1,0:T(8,128)(2,1)} %bitcast.55, bf16[1,1536,1536]{2,1,0:T(8,128)(2,1)} %all-gather.8.cloned.1.call-done), kind=kOutput, calls=%fused_computation.1 | convolution fusion | flops 6041763840 | bytes 12582912 | tf_op jit(solution)/shard_map/dot_general | solution.py:52
  161.7 239.2 %all-reduce.6 = f32[1280,1536]{1,0:T(8,128)} all-reduce(bf16[1280,1536]{1,0:T(8,128)(2,1)} %convolution_convert_fusion), channel_id=1, replica_groups=mesh['teacher'=4,'seq'=32] {'teacher'}, use_global_device_ids=true, to_apply=%region_4.0 | all-reduce | flops 1966080 | bytes 11796480 | tf_op jit(solution)/shard_map/psum | solution.py:58
  400.9 2.7 fusion.3
  403.6 0.0 copy-done.5
  403.6 2.6 fusion.2
  406.2 0.0 copy-done.3
  406.2 3.6 fusion.21
  409.8 60.0 %all-gather.6.cloned.1.call-done = bf16[768,1536]{1,0:T(8,128)(2,1)} async-done(((bf16[24,1536]{1,0:T(8,128)(2,1)}), bf16[768,1536]{1,0:T(8,128)(2,1)}) %all-gather.6.cloned.1.call-update) | async-done | bytes 2359312 | tf_op jit(solution)/shard_map/all_gather | solution.py:88
  469.8 4.4 multiply_reduce_fusion
  474.2 0.0 copy-done.1
  474.2 3.7 fusion.28
  477.9 0.0 reduce-scatter.5.cloned.1.call-update
  478.0 0.2 reduce-scatter.3.cloned.1.call-start
  478.2 0.8 fusion.14
  479.0 0.4 copy-done.2
  479.4 3.0 fusion.22
  482.4 3.6 convolution_bitcast_fusion
  486.0 0.0 copy-done.4
  486.0 3.6 convolution_bitcast_fusion.2
  489.6 3.7 convolution_bitcast_fusion.1
  493.3 11.1 %pad_maximum_fusion = f32[1536,3,768]{2,0,1:T(8,128)} fusion(f32[1536,1,768]{2,0,1:T(8,128)} %convolution_bitcast_fusion, f32[1536,1,768]{2,0,1:T(8,128)} %convolution_bitcast_fusion.1, f32[1536,1,768]{2,0,1:T(8,128)} %convolution_bitcast_fusion.2), kind=kLoop, calls=%fused_computation | loop fusion | flops 7077888 | bytes 28311552 | tf_op jit(solution)/shard_map/stack | solution.py:99
  504.3 0.0 reduce-scatter.3.cloned.1.call-update
  504.3 0.0 all-reduce.5.cloned.1.call-start
  504.4 145.1 %reduce-scatter.5.cloned.1.call-done = f32[24,1536]{1,0:T(8,128)} async-done(((f32[768,1536]{1,0:T(8,128)}), f32[24,1536]{1,0:T(8,128)}) %reduce-scatter.5.cloned.1.call-update) | async-done | bytes 147472 | tf_op jit(solution)/shard_map/reduce_scatter | solution.py:107
  649.5 194.7 %reduce-scatter.3.cloned.1.call-done = f32[48,3,768]{2,0,1:T(8,128)} async-done(((f32[1536,3,768]{2,0,1:T(8,128)}), f32[48,3,768]{2,0,1:T(8,128)}) %reduce-scatter.3.cloned.1.call-update) | async-done | bytes 442384 | tf_op jit(solution)/shard_map/reduce_scatter | solution.py:98
  844.2 0.0 all-reduce.5.cloned.1.call-update
  844.2 84.7 %psum.45 = f32[]{:T(128)} all-reduce(f32[]{:T(128)} %get-tuple-element.15), channel_id=1, replica_groups=mesh['teacher'=4,'seq'=32] {'teacher','seq'}, use_global_device_ids=true, to_apply=%region_6.0 | all-reduce | flops 1 | bytes 8 | tf_op jit(solution)/shard_map/psum | solution.py:91
  929.6 0.0 all-reduce.5.cloned.1.call-done
  929.6 1.8 copy.12
  931.4 1.6 copy.13
  (10 shorter events, 0.1 us)
Async XLA Ops:
  7.2 74.5 %copy-start = (bf16[5,64,1536]{2,1,0:T(8,128)(2,1)S(1)}, bf16[5,64,1536]{2,1,0:T(8,128)(2,1)}, u32[]{:S(2)}) copy-start(bf16[5,64,1536]{2,1,0:T(8,128)(2,1)} %param.5) | copy-start | bytes 2949124
  7.2 143.8 %all-gather.8.cloned.1.call-start = ((), (), s32[]{:S(2)}) async-start(), calls=%async_computation.4 | async-start | bytes 4866048 | tf_op jit(solution)/shard_map/all_gather | solution.py:54
  7.9 393.0 %all-gather.4.cloned.1.call-start = ((), (), s32[]{:S(2)}) async-start(), calls=%async_computation.2 | async-start | bytes 7299072 | tf_op jit(solution)/shard_map/all_gather | solution.py:81
  8.7 461.1 %all-gather.6.cloned.1.call-start = ((), (), s32[]{:S(2)}) async-start(), calls=%async_computation.3 | async-start | bytes 2433024 | tf_op jit(solution)/shard_map/all_gather | solution.py:88
  82.6 8.4 collective-permute-start
  83.9 11.4 %collective-permute-start.1 = (bf16[5,16,1536]{2,1,0:T(8,128)(2,1)S(1)}, bf16[5,16,1536]{2,1,0:T(8,128)(2,1)S(1)}, u32[]{:S(2)}, u32[]{:S(2)}) collective-permute-start(bf16[5,16,1536]{2,1,0:T(8,128)(2,1)S(1)} %get-tuple-element.12), channel_id=1, source_target_pairs={{1,0},{2,1},{3,2},{4,3},{5,4},{6,5},{7,6},{8,7},{9,8},{10,9},{11,1... | collective-permute-start | bytes 737288 | tf_op jit(solution)/shard_map/ppermute | solution.py:19
  85.2 564.3 %reduce-scatter.5.cloned.1.call-start = ((), (), s32[]{:S(2)}) async-start(), calls=%async_computation.6 | async-start | bytes 4866048 | tf_op jit(solution)/shard_map/reduce_scatter | solution.py:107
  96.4 309.8 %copy-start.3 = (bf16[5,64,1536]{2,1,0:T(8,128)(2,1)}, bf16[5,64,1536]{2,1,0:T(8,128)(2,1)S(1)}, u32[]{:S(2)}) copy-start(bf16[5,64,1536]{2,1,0:T(8,128)(2,1)S(1)} %get-tuple-element.9) | copy-start | bytes 2949124
  400.9 2.7 copy-start.5
  469.8 4.4 copy-start.1
  478.0 366.2 %reduce-scatter.3.cloned.1.call-start = ((), (), s32[]{:S(2)}) async-start(), calls=%async_computation.5 | async-start | bytes 14598144 | tf_op jit(solution)/shard_map/reduce_scatter | solution.py:98
  478.2 1.2 copy-start.2
  479.4 3.0 copy-start.6
  482.4 3.6 copy-start.4
  504.3 425.2 %all-reduce.5.cloned.1.call-start = ((), (), s32[]{:S(2)}) async-start(), calls=%async_computation.7 | async-start | bytes 1179648 | tf_op jit(solution)/shard_map/psum | solution.py:110
Sparse Core Ops, SparseCore 0:
  9.6 141.3 all-gather.7
  152.6 172.9 all-gather.3
  327.3 142.4 all-gather.5
  478.1 171.3 reduce-scatter.4
  651.8 192.3 reduce-scatter.2
  846.6 61.8 all-reduce.4
where the time goes:
time: 941 us
  waiting for transfers between devices  466 us (50%)
  blocking collectives  395 us (42%)
  matrix products  41.5 us (4%)
  between operations  16 us (2%)
  other arithmetic  15.3 us (2%)
    psum x1, blocking collectives, shards(): summed = lax.psum(projected, 'teacher')  239 us
    reduce_scatter x1, waiting for transfers between devices, shards(): lax.psum_scatter(jnp.stack([column_product(tap_weights[offset_index], pre...  195 us
    reduce_scatter x1, waiting for transfers between devices, shards(): lax.psum_scatter(column_product(activated, out_grad), 'seq', scatter_dime...  145 us
    psum x1, blocking collectives, shards(): squared_total = lax.psum(jnp.sum(misfit * misfit), ('teacher', 'seq'))  84.7 us
    psum x1, blocking collectives, shards(): lax.psum((jnp.sum(inputs_f, axis=0), jnp.sum(inputs_f * inputs_f, axis=0)...  71.5 us
    all_gather x1, waiting for transfers between devices, shards(): pointwise_full = lax.all_gather(pointwise_weight, 'seq', axis=0, tiled=True)  60 us
    all_gather x1, waiting for transfers between devices, shards(): lax.all_gather(projection, 'seq', axis=1, tiled=True)[0]  54.6 us
  transfers between devices with their start and end apart: 8, of which 6 were waited for; matrix products, arithmetic and copies ran while one was open for 5% of the time, Pallas kernels for 0%

commit v1 on v0

--- a/solution.py
+++ b/solution.py
@@ -62,7 +62,8 @@
     target = own_rows / groups
     inputs_f = activations.reshape(count_of_rows, channel_count).astype(jnp.float32)
     sum_first, sum_second = lax.psum(
-        (jnp.sum(inputs_f, axis=0), jnp.sum(inputs_f * inputs_f, axis=0)), ("teacher", "seq")
+        lax.psum((jnp.sum(inputs_f, axis=0), jnp.sum(inputs_f * inputs_f, axis=0)), "teacher"),
+        "seq",
     )
     channel_mean = sum_first / total_rows
     channel_var = sum_second / total_rows - channel_mean * channel_mean

time: 941 us -> 1020 us (1.084)
  blocking collectives: 395 us -> 454 us
  waiting for transfers between devices: 466 us -> 487 us
    all_gather x1, waiting for transfers between devices: 54.6 us -> 139 us  [shards(): lax.all_gather(projection, 'seq', axis=1, tiled=True)[0]]
    all_gather x1, waiting for transfers between devices: 60 us -> 0.01 us  [shards(): pointwise_full = lax.all_gather(pointwise_weight, 'seq', axis=0, tiled=True)]
    psum x1, blocking collectives: 71.5 us -> 128 us  [shards(): lax.psum(lax.psum((jnp.sum(inputs_f, axis=0), jnp.sum(inputs_f * inputs_f...]
  transfers between devices with their start and end apart: 8 -> 8, of which waited for: 6 -> 5; matrix products, arithmetic and copies ran while one was open for 5% -> 5% of each run, Pallas kernels for 0% -> 0%
where the time goes in v1:
time: 1020 us
  waiting for transfers between devices  487 us (48%)
  blocking collectives  454 us (45%)
  matrix products  41.8 us (4%)
  between operations  16 us (2%)
  other arithmetic  15.3 us (2%)
    psum x1, blocking collectives, shards(): summed = lax.psum(projected, 'teacher')  242 us
    reduce_scatter x1, waiting for transfers between devices, shards(): lax.psum_scatter(jnp.stack([column_product(tap_weights[offset_index], pre...  195 us
    reduce_scatter x1, waiting for transfers between devices, shards(): lax.psum_scatter(column_product(activated, out_grad), 'seq', scatter_dime...  145 us
    all_gather x1, waiting for transfers between devices, shards(): lax.all_gather(projection, 'seq', axis=1, tiled=True)[0]  139 us
    psum x1, blocking collectives, shards(): lax.psum(lax.psum((jnp.sum(inputs_f, axis=0), jnp.sum(inputs_f * inputs_f...  128 us
    psum x1, blocking collectives, shards(): squared_total = lax.psum(jnp.sum(misfit * misfit), ('teacher', 'seq'))  83.7 us
  transfers between devices with their start and end apart: 8, of which 5 were waited for; matrix products, arithmetic and copies ran while one was open for 5% of the time, Pallas kernels for 0%

profile of v1, /device:TPU:1, one launch (start us, length us, event | category | flops | bytes accessed | tf_op | source)
XLA Modules:
  0.0 1020.4 jit_solution(11179364586063461192)
XLA Ops:
  7.2 0.0 all-gather.8.cloned.1.call-start
  7.2 0.7 all-gather.8.cloned.1.call-update
  7.9 0.0 all-gather.4.cloned.1.call-start
  7.9 0.7 all-gather.4.cloned.1.call-update
  8.6 0.0 all-gather.6.cloned.1.call-start
  8.7 0.7 all-gather.6.cloned.1.call-update
  9.4 0.0 reduce-scatter.5.cloned.1.call-start
  9.4 1.5 convert_reduce_fusion
  10.9 139.2 %all-gather.8.cloned.1.call-done = bf16[1,1536,1536]{2,1,0:T(8,128)(2,1)} async-done(((bf16[1,48,1536]{2,1,0:T(8,128)(2,1)}), bf16[1,1536,1536]{2,1,0:T(8,128)(2,1)}) %all-gather.8.cloned.1.call-update) | async-done | bytes 4718608 | tf_op jit(solution)/shard_map/all_gather | solution.py:54
  150.1 10.6 %convolution_convert_fusion = bf16[1280,1536]{1,0:T(8,128)(2,1)} fusion(bf16[1280,1536]{1,0:T(8,128)(2,1)} %bitcast.55, bf16[1,1536,1536]{2,1,0:T(8,128)(2,1)} %all-gather.8.cloned.1.call-done), kind=kOutput, calls=%fused_computation.1 | convolution fusion | flops 6041763840 | bytes 12582912 | tf_op jit(solution)/shard_map/dot_general | solution.py:52
  160.8 241.8 %all-reduce.7 = (f32[1280,1536]{1,0:T(8,128)}, f32[1536]{0:T(1024)S(1)}, f32[1536]{0:T(1024)S(1)}) all-reduce(bf16[1280,1536]{1,0:T(8,128)(2,1)} %convolution_convert_fusion, f32[1536]{0:T(1024)S(1)} %get-tuple-element.4, f32[1536]{0:T(1024)S(1)} %get-tuple-element.3), channel_id=1, replica_groups=mesh['teacher'=4,'seq'=32] {'teacher'}, use_global_device_ids=true, to_apply=%region_6.0 | all-reduce | flops 1969152 | bytes 11821056 | tf_op jit(solution)/shard_map/psum | solution.py:58
  402.6 128.0 %all-reduce = (f32[1536]{0:T(1024)S(1)}, f32[1536]{0:T(1024)S(1)}) all-reduce(f32[1536]{0:T(1024)S(1)} %get-tuple-element.8, f32[1536]{0:T(1024)S(1)} %get-tuple-element.9), channel_id=1, replica_groups=mesh['teacher'=4,'seq'=32] {'seq'}, use_global_device_ids=true, to_apply=%region_5.0 | all-reduce | flops 3072 | bytes 24576 | tf_op jit(solution)/shard_map/psum | solution.py:64
  530.6 0.0 copy-done
  530.6 0.8 fusion.9
  531.5 1.3 collective-permute-start
  532.8 1.3 collective-permute-start.1
  534.1 1.8 collective-permute-done
  535.9 3.8 collective-permute-done.1
  539.7 1.1 pad_maximum_fusion.2
  540.9 3.0 fusion.3
  543.9 0.0 copy-done.5
  543.9 2.6 fusion.2
  546.5 0.0 copy-done.3
  546.5 3.6 fusion.21
  550.1 4.4 multiply_reduce_fusion
  554.5 0.0 copy-done.1
  554.5 3.7 fusion.28
  558.2 0.0 reduce-scatter.5.cloned.1.call-update
  558.3 0.2 reduce-scatter.3.cloned.1.call-start
  558.5 0.0 copy-start.2
  558.5 0.8 fusion.14
  559.3 0.4 copy-done.2
  559.7 3.0 fusion.22
  562.7 0.0 copy-done.6
  562.7 0.0 copy-start.4
  562.8 3.6 convolution_bitcast_fusion
  566.3 3.6 convolution_bitcast_fusion.2
  569.9 3.7 convolution_bitcast_fusion.1
  573.6 11.1 %pad_maximum_fusion = f32[1536,3,768]{2,0,1:T(8,128)} fusion(f32[1536,1,768]{2,0,1:T(8,128)} %convolution_bitcast_fusion, f32[1536,1,768]{2,0,1:T(8,128)} %convolution_bitcast_fusion.1, f32[1536,1,768]{2,0,1:T(8,128)} %convolution_bitcast_fusion.2), kind=kLoop, calls=%fused_computation | loop fusion | flops 7077888 | bytes 28311552 | tf_op jit(solution)/shard_map/stack | solution.py:100
  584.6 0.0 reduce-scatter.3.cloned.1.call-update
  584.6 0.0 all-reduce.6.cloned.1.call-start
  584.7 144.9 %reduce-scatter.5.cloned.1.call-done = f32[24,1536]{1,0:T(8,128)} async-done(((f32[768,1536]{1,0:T(8,128)}), f32[24,1536]{1,0:T(8,128)}) %reduce-scatter.5.cloned.1.call-update) | async-done | bytes 147472 | tf_op jit(solution)/shard_map/reduce_scatter | solution.py:108
  729.6 195.0 %reduce-scatter.3.cloned.1.call-done = f32[48,3,768]{2,0,1:T(8,128)} async-done(((f32[1536,3,768]{2,0,1:T(8,128)}), f32[48,3,768]{2,0,1:T(8,128)}) %reduce-scatter.3.cloned.1.call-update) | async-done | bytes 442384 | tf_op jit(solution)/shard_map/reduce_scatter | solution.py:99
  924.6 0.0 all-reduce.6.cloned.1.call-update
  924.6 83.7 %psum.61 = f32[]{:T(128)} all-reduce(f32[]{:T(128)} %get-tuple-element.18), channel_id=1, replica_groups=mesh['teacher'=4,'seq'=32] {'teacher','seq'}, use_global_device_ids=true, to_apply=%region_8.0 | all-reduce | flops 1 | bytes 8 | tf_op jit(solution)/shard_map/psum | solution.py:92
  1009.0 0.0 all-reduce.6.cloned.1.call-done
  1009.0 1.8 copy.14
  1010.9 1.6 copy.15
  (10 shorter events, 0.1 us)
Async XLA Ops:
  7.2 143.0 %all-gather.8.cloned.1.call-start = ((), (), s32[]{:S(2)}) async-start(), calls=%async_computation.4 | async-start | bytes 4866048 | tf_op jit(solution)/shard_map/all_gather | solution.py:54
  7.9 533.0 %all-gather.4.cloned.1.call-start = ((), (), s32[]{:S(2)}) async-start(), calls=%async_computation.2 | async-start | bytes 7299072 | tf_op jit(solution)/shard_map/all_gather | solution.py:82
  8.6 541.4 %all-gather.6.cloned.1.call-start = ((), (), s32[]{:S(2)}) async-start(), calls=%async_computation.3 | async-start | bytes 2433024 | tf_op jit(solution)/shard_map/all_gather | solution.py:89
  9.4 720.2 %reduce-scatter.5.cloned.1.call-start = ((), (), s32[]{:S(2)}) async-start(), calls=%async_computation.6 | async-start | bytes 4866048 | tf_op jit(solution)/shard_map/reduce_scatter | solution.py:108
  160.8 369.8 %copy-start = (bf16[5,64,1536]{2,1,0:T(8,128)(2,1)S(1)}, bf16[5,64,1536]{2,1,0:T(8,128)(2,1)}, u32[]{:S(2)}) copy-start(bf16[5,64,1536]{2,1,0:T(8,128)(2,1)} %param.5) | copy-start | bytes 2949124
  531.5 4.4 collective-permute-start
  532.8 6.9 collective-permute-start.1
  540.9 5.6 copy-start.3
  540.9 3.0 copy-start.5
  550.1 4.4 copy-start.1
  558.3 366.3 %reduce-scatter.3.cloned.1.call-start = ((), (), s32[]{:S(2)}) async-start(), calls=%async_computation.5 | async-start | bytes 14598144 | tf_op jit(solution)/shard_map/reduce_scatter | solution.py:99
  558.5 1.2 copy-start.2
  559.7 3.0 copy-start.6
  562.7 3.6 copy-start.4
  584.6 424.4 %all-reduce.6.cloned.1.call-start = ((), (), s32[]{:S(2)}) async-start(), calls=%async_computation.7 | async-start | bytes 1179648 | tf_op jit(solution)/shard_map/psum | solution.py:111
Sparse Core Ops, SparseCore 0:
  9.6 140.4 all-gather.7
  151.8 173.2 all-gather.3
  326.8 142.8 all-gather.5
  558.4 171.1 reduce-scatter.4
  731.9 192.6 reduce-scatter.2
  927.0 61.3 all-reduce.5
